TPU v7x, 256 devices: a whole 4x4x8 slice. The times are simulated.
256 devices in a mesh: dp: 8 (over z_lo, core), heads: 32 (over y, x, z_hi).
Axes of the slice: x: 4, y: 4, z: 8 (z_hi: 2, z_lo: 4; z = z_hi * 4 + z_lo), core: 2. Of those that a mesh axis runs over, the one named last changes fastest.
Arguments:
- latent: bfloat16 [8, 1024, 512], P(None, 'dp'), may hold values from -6 to 6
- rope_keys: bfloat16 [8, 1024, 64], P(None, 'dp'), may hold values from -6 to 6
- queries: bfloat16 [8, 1024, 24576], P(None, 'dp', 'heads'), may hold values from -320 to 320
- grad_out: bfloat16 [8, 1024, 16384], P(None, 'dp', 'heads'), may hold values from -2 to 2
- key_value_up_weight: bfloat16 [8, 512, 32768], P('dp', None, 'heads'), may hold values from -0.25 to 0.25
- momentum: bfloat16 [8, 512, 32768], P('dp', None, 'heads'), may hold values from -16 to 16
Outputs:
- new_momentum: bfloat16 [8, 512, 32768], P('dp', None, 'heads')
- layer_update_step: float32 [8, 512, 32768], P('dp', None, 'heads')
All inputs are finite; a program needn't handle non-finite values.
Results may differ from a plain program's by a relative error of at most 0.015.
Values may be sent and summed in bfloat16 or wider, within the bound.
No kernel may reach another device: no remote copies, remote signals or barrier semaphores. Data moves between devices by JAX's collectives and lax.ppermute only.
A program may use at most 64 MiB of HBM per device.

v0:
```python
import math
import jax
import jax.numpy as jnp
from jax import lax
from jax.sharding import PartitionSpec as P

LATENT = 512
HEADS = 128
NOPE = 128
ROPE = 64
VDIM = 128
STEPS = 2
poly_first = 3.4445
poly_second = -4.775
poly_third = 2.0315
norm_epsilon = 1e-07
decay_rate = 0.95


def layer_grads(compressed_latent_rows, rotary_position_rows, query_rows, grad_rows, weight_cols):
    rows = compressed_latent_rows.shape[0]
    heads_here = query_rows.shape[1] // (NOPE + ROPE)
    score_scale = 1.0 / math.sqrt(NOPE + ROPE)
    kv_rows = jnp.dot(
        compressed_latent_rows, weight_cols, preferred_element_type=jnp.float32
    ).astype(jnp.bfloat16)
    kv_rows = kv_rows.reshape(rows, heads_here, NOPE + VDIM)
    key_nope = kv_rows[:, :, :NOPE]
    values = kv_rows[:, :, NOPE:]
    query_all = query_rows.reshape(rows, heads_here, NOPE + ROPE)
    query_nope = query_all[:, :, :NOPE]
    query_rope = query_all[:, :, NOPE:]
    scores = jnp.einsum("shd,thd->hst", query_nope, key_nope, preferred_element_type=jnp.float32)
    scores = scores + jnp.einsum(
        "shd,td->hst", query_rope, rotary_position_rows, preferred_element_type=jnp.float32
    )
    scores = scores * score_scale
    places = jnp.arange(rows)
    allowed = places[None, :] <= places[:, None]
    scores = jnp.where(allowed[None], scores, -jnp.inf)
    top_score = jnp.max(scores, axis=-1, keepdims=True)
    expd = jnp.exp(scores - top_score)
    probs = expd / jnp.sum(expd, axis=-1, keepdims=True)
    probs_low = probs.astype(jnp.bfloat16)
    grad_heads = grad_rows.reshape(rows, heads_here, VDIM)
    grad_values = jnp.einsum(
        "hst,shd->thd", probs_low, grad_heads, preferred_element_type=jnp.float32
    )
    grad_probs = jnp.einsum("shd,thd->hst", grad_heads, values, preferred_element_type=jnp.float32)
    row_delta = jnp.sum(probs * grad_probs, axis=-1, keepdims=True)
    grad_scores = (probs * (grad_probs - row_delta) * score_scale).astype(jnp.bfloat16)
    grad_keys = jnp.einsum(
        "hst,shd->thd", grad_scores, query_nope, preferred_element_type=jnp.float32
    )
    joined = jnp.concatenate([grad_keys, grad_values], axis=-1).astype(jnp.bfloat16)
    return joined.reshape(rows, heads_here * (NOPE + VDIM))


def body(latent, rope_keys, queries, grad_out, key_value_up_weight, momentum):
    highest = lax.Precision.HIGHEST
    weights_all = lax.all_gather(key_value_up_weight, "dp", axis=0, tiled=True)

    def layer_body(carry, inputs):
        return (carry, layer_grads(inputs[0], inputs[1], inputs[2], inputs[3], inputs[4]))

    unused, key_value_gradient_total = lax.scan(
        layer_body, 0, (latent, rope_keys, queries, grad_out, weights_all)
    )
    grads = lax.psum_scatter(
        jnp.einsum(
            "eot,eov->etv", latent, key_value_gradient_total, preferred_element_type=jnp.float32
        ).astype(jnp.bfloat16),
        "dp",
        scatter_dimension=0,
        tiled=True,
    ).astype(jnp.float32)
    fresh = (decay_rate * momentum.astype(jnp.float32) + grads).astype(jnp.bfloat16)
    source = fresh[0].astype(jnp.float32)
    squares = lax.psum(jnp.sum(source * source), "heads")
    norm_value = jnp.sqrt(squares) + norm_epsilon
    iterate = source / norm_value
    for count_index in range(STEPS):
        gram = lax.psum(
            jnp.dot(iterate, iterate.T, precision=highest).astype(jnp.bfloat16), "heads"
        ).astype(jnp.float32)
        poly = poly_second * gram + poly_third * jnp.dot(gram, gram, precision=highest)
        iterate = poly_first * iterate + jnp.dot(poly, iterate, precision=highest)
    update_scale = 0.2 * math.sqrt(max(LATENT, HEADS * (NOPE + VDIM)))
    return (fresh, (update_scale * iterate)[None])


def solution(mesh):
    placed = (
        P(None, "dp", None),
        P(None, "dp", None),
        P(None, "dp", "heads"),
        P(None, "dp", "heads"),
        P("dp", None, "heads"),
        P("dp", None, "heads"),
    )
    return jax.shard_map(
        body,
        mesh=mesh,
        in_specs=placed,
        out_specs=(P("dp", None, "heads"), P("dp", None, "heads")),
        check_vma=False,
    )
```

profile of v0, /device:TPU:32, one launch (start us, length us, event | category | flops | bytes accessed | tf_op | source)
XLA Modules:
  0.0 1253.7 jit_solution(448452427187309342)
XLA Ops:
  7.2 0.7 all-gather.2.cloned.1.call-update
  8.0 94.5 %all-gather.2.cloned.1.call-done = bf16[8,512,1024]{2,1,0:T(8,128)(2,1)} async-done(((bf16[1,512,1024]{2,1,0:T(8,128)(2,1)}), bf16[8,512,1024]{2,1,0:T(8,128)(2,1)}) %all-gather.2.cloned.1.call-update) | async-done | bytes 8388624 | tf_op jit(solution)/shard_map/all_gather | solution.py:61
  102.4 49.9 %while.10 = (s32[]{:T(128)}, bf16[8,128,1024]{1,2,0:T(8,128)(2,1)S(1)}, bf16[8,128,768]{2,1,0:T(8,128)(2,1)}, bf16[8,128,512]{2,1,0:T(8,128)(2,1)}, bf16[8,512,1...) while((s32[]{:T(128)}, ...), condition=%wide.region_4.5_spmd, body=%wide.region_0.4_spmd.sunk | while | flops 211502464 | bytes 8906337 | solution.py:66
  102.4 0.9 constant_dynamic-slice_fusion.5
  103.5 0.9 convolution_bitcast_fusion.2
  104.5 1.6 convolution_convert_fusion.4
  106.6 0.2 fusion.99
  106.8 0.9 constant_dynamic-slice_fusion.4
  108.1 0.2 fusion.102
  108.7 0.9 constant_dynamic-slice_fusion.5
  109.8 0.9 convolution_bitcast_fusion.2
  110.7 1.6 convolution_convert_fusion.4
  112.8 0.2 fusion.99
  113.1 0.9 constant_dynamic-slice_fusion.4
  114.3 0.2 fusion.102
  114.9 0.9 constant_dynamic-slice_fusion.5
  116.0 0.9 convolution_bitcast_fusion.2
  117.0 1.6 convolution_convert_fusion.4
  119.1 0.2 fusion.99
  119.3 0.9 constant_dynamic-slice_fusion.4
  120.6 0.2 fusion.102
  121.2 0.9 constant_dynamic-slice_fusion.5
  122.3 0.9 convolution_bitcast_fusion.2
  123.2 1.6 convolution_convert_fusion.4
  125.3 0.2 fusion.99
  125.6 0.9 constant_dynamic-slice_fusion.4
  126.8 0.2 fusion.102
  127.4 0.9 constant_dynamic-slice_fusion.5
  128.5 0.9 convolution_bitcast_fusion.2
  129.4 1.6 convolution_convert_fusion.4
  131.6 0.2 fusion.99
  131.8 0.9 constant_dynamic-slice_fusion.4
  133.0 0.2 fusion.102
  133.6 0.9 constant_dynamic-slice_fusion.5
  134.7 0.9 convolution_bitcast_fusion.2
  135.7 1.6 convolution_convert_fusion.4
  138.0 0.9 constant_dynamic-slice_fusion.4
  139.3 0.2 fusion.102
  139.9 0.9 constant_dynamic-slice_fusion.5
  141.0 0.9 convolution_bitcast_fusion.2
  141.9 1.6 convolution_convert_fusion.4
  144.3 0.9 constant_dynamic-slice_fusion.4
  145.5 0.2 fusion.102
  146.1 0.9 constant_dynamic-slice_fusion.5
  147.2 0.9 convolution_bitcast_fusion.2
  148.2 1.6 convolution_convert_fusion.4
  150.5 0.9 constant_dynamic-slice_fusion.4
  151.8 0.2 fusion.102
  152.3 6.8 convert_bitcast_fusion
  159.2 1.1 copy-done
  160.3 0.5 copy.41
  160.9 91.8 %reduce-scatter.2.cloned.1.call-done = bf16[1,512,1024]{1,2,0:T(8,128)(2,1)} async-done(((bf16[8,512,1024]{1,2,0:T(8,128)(2,1)}), bf16[1,512,1024]{1,2,0:T(8,128)(2,1)}) %reduce-scatter.2.cloned.1.call-update) | async-done | bytes 1048592 | tf_op jit(solution)/shard_map/reduce_scatter | solution.py:69
  252.7 2.4 fusion.34
  255.1 119.8 %psum.21 = f32[]{:T(128)} all-reduce(f32[]{:T(128)} %get-tuple-element.74), channel_id=1, replica_groups=mesh['dp'=8,'heads'=32] {'heads'}, use_global_device_ids=true, to_apply=%region_7.8 | all-reduce | flops 1 | bytes 8 | tf_op jit(solution)/shard_map/psum | solution.py:79
  375.6 4.4 fusion.41
  380.3 419.3 %all-reduce.3.cloned.1.call-done = bf16[512,512]{1,0:T(8,128)(2,1)} async-done(((bf16[512,512]{1,0:T(8,128)(2,1)}), bf16[512,512]{1,0:T(8,128)(2,1)}) %all-reduce.3.cloned.1.call-update) | async-done | bytes 524304 | tf_op jit(solution)/shard_map/psum | solution.py:83
  799.6 1.8 fusion.40
  801.4 3.6 multiply_add_fusion
  805.0 4.3 convolution_convert_fusion.2
  809.4 1.3 copy.46
  810.7 426.9 %all-reduce.5.cloned.1.call-done = bf16[512,512]{1,0:T(8,128)(2,1)} async-done(((bf16[512,512]{1,0:T(8,128)(2,1)}), bf16[512,512]{1,0:T(8,128)(2,1)}) %all-reduce.5.cloned.1.call-update) | async-done | bytes 524304 | tf_op jit(solution)/shard_map/psum | solution.py:83
  1237.5 1.8 fusion.39
  1239.4 4.9 multiply_bitcast_fusion
  1244.3 2.9 copy.47
  (92 shorter events, 10.9 us)
Async XLA Ops:
  7.2 95.3 %all-gather.2.cloned.1.call-start = ((), (), s32[]{:S(2)}) async-start(), calls=%async_computation.1 | async-start | bytes 9437184 | tf_op jit(solution)/shard_map/all_gather | solution.py:61
  7.9 244.8 %reduce-scatter.2.cloned.1.call-start = ((), (), s32[]{:S(2)}) async-start(), calls=%async_computation.2 | async-start | bytes 9437184 | tf_op jit(solution)/shard_map/reduce_scatter | solution.py:69
  159.1 1.2 copy-start
  159.2 640.5 %all-reduce.3.cloned.1.call-start = ((), (), s32[]{:S(2)}) async-start(), calls=%async_computation.3 | async-start | bytes 1048576 | tf_op jit(solution)/shard_map/psum | solution.py:83
  380.1 857.5 %all-reduce.5.cloned.1.call-start = ((), (), s32[]{:S(2)}) async-start(), calls=%async_computation.4 | async-start | bytes 1048576 | tf_op jit(solution)/shard_map/psum | solution.py:83
Sparse Core Ops, SparseCore 0:
  9.8 92.6 all-gather.1
  159.3 93.3 reduce-scatter.1
  380.2 419.3 all-reduce.2
  809.5 428.0 all-reduce.4
where the time goes:
time: 1260 us; the launch traced here: 1250 us
  waiting for transfers between devices  1030 us (82%)
  blocking collectives  120 us (10%)
  matrix products  54.8 us (4%)
  local copies, waits for them, and re-layouts  25.5 us (2%)
  between operations  14.5 us (1%)
    psum x2, waiting for transfers between devices, body(): lax.psum(jnp.dot(iterate, iterate.T, precision=highest).astype(jnp.bfloat...  846 us
    psum x1, blocking collectives, body(): squares = lax.psum(jnp.sum(source * source), 'heads')  120 us
    all_gather x1, waiting for transfers between devices, body(): weights_all = lax.all_gather(key_value_up_weight, 'dp', axis=0, tiled=True)  94.5 us
    reduce_scatter x1, waiting for transfers between devices, body(): lax.psum_scatter(jnp.einsum('eot,eov->etv', latent, key_value_gradient_to...  91.8 us
  transfers between devices with their start and end apart: 4, of which 4 were waited for; matrix products, arithmetic and copies ran while one was open for 0% of the time, Pallas kernels for 0%

commit v1 on v0

--- a/solution.py
+++ b/solution.py
@@ -58,7 +58,8 @@
 
 def body(latent, rope_keys, queries, grad_out, key_value_up_weight, momentum):
     highest = lax.Precision.HIGHEST
-    weights_all = lax.all_gather(key_value_up_weight, "dp", axis=0, tiled=True)
+    repeated = jnp.stack([key_value_up_weight] * lax.axis_size("dp"))
+    weights_all = jnp.concatenate(lax.all_to_all(repeated, "dp", 0, 0), axis=0)
 
     def layer_body(carry, inputs):
         return (carry, layer_grads(inputs[0], inputs[1], inputs[2], inputs[3], inputs[4]))

time: 1260 us -> 1360 us (1.079)
  waiting for transfers between devices: 1030 us -> 1120 us
    all_to_all x0 -> x1, waiting for transfers between devices: none -> 180 us  [body(): weights_all = jnp.concatenate(lax.all_to_all(repeated, 'dp', 0, 0), axis=0)]
    all_gather x1 -> x0, waiting for transfers between devices: 94.5 us -> none  [body(): weights_all = lax.all_gather(key_value_up_weight, 'dp', axis=0, tiled=True)]
where the time goes in v1:
time: 1360 us
  waiting for transfers between devices  1120 us (82%)
  blocking collectives  120 us (9%)
  matrix products  54.5 us (4%)
  local copies, waits for them, and re-layouts  36.5 us (3%)
  between operations  14.5 us (1%)
    psum x2, waiting for transfers between devices, body(): lax.psum(jnp.dot(iterate, iterate.T, precision=highest).astype(jnp.bfloat...  846 us
    all_to_all x1, waiting for transfers between devices, body(): weights_all = jnp.concatenate(lax.all_to_all(repeated, 'dp', 0, 0), axis=0)  180 us
    psum x1, blocking collectives, body(): squares = lax.psum(jnp.sum(source * source), 'heads')  120 us
    reduce_scatter x1, waiting for transfers between devices, body(): lax.psum_scatter(jnp.einsum('eot,eov->etv', latent, key_value_gradient_to...  93.8 us
  transfers between devices with their start and end apart: 4, of which 4 were waited for; matrix products, arithmetic and copies ran while one was open for 0% of the time, Pallas kernels for 0%

profile of v1, /device:TPU:32, one launch (start us, length us, event | category | flops | bytes accessed | tf_op | source)
XLA Modules:
  0.0 1358.1 jit_solution(15985667567111436438)
XLA Ops:
  7.2 5.5 stack.2
  12.7 6.8 all-to-all-start
  19.5 180.4 %all-to-all-done = bf16[8,1,512,1024]{3,2,1,0:T(8,128)(2,1)} async-done(((bf16[8,1,512,1024]{3,2,1,0:T(8,128)(2,1)}), bf16[8,1,512,1024]{3,2,1,0:T(8,128)(2,1)}, u32[]{:S(2)}, u32[]{:S(2)}) %all-to-all-start) | async-done | bytes 8388640 | tf_op jit(solution)/shard_map/all_to_all | solution.py:62
  199.9 54.6 %while.10 = (s32[]{:T(128)}, bf16[8,128,1024]{1,2,0:T(8,128)(2,1)}, bf16[8,128,768]{2,1,0:T(8,128)(2,1)}, bf16[8,128,512]{2,1,0:T(8,128)(2,1)S(1)}, bf16[8,512,1...) while((s32[]{:T(128)}, bf16[8,128,1024]{1,2,0:T(8,128)(2,1)}, ...), condition=%wide.region_4.5_spmd, body=%wide.region_0.4_spmd.sunk | while | flops 211502464 | bytes 8906845 | solution.py:67
  199.9 0.9 constant_dynamic-slice_fusion.5
  201.0 0.9 convolution_bitcast_fusion.2
  201.9 1.5 convolution_convert_fusion.4
  204.2 0.9 constant_dynamic-slice_fusion.4
  205.5 0.2 fusion.102
  206.0 0.7 constant_dynamic-update-slice_fusion.2
  206.7 0.9 constant_dynamic-slice_fusion.5
  207.8 0.9 convolution_bitcast_fusion.2
  208.8 1.5 convolution_convert_fusion.4
  211.1 0.9 constant_dynamic-slice_fusion.4
  212.8 0.7 constant_dynamic-update-slice_fusion.2
  213.5 0.9 constant_dynamic-slice_fusion.5
  214.6 0.9 convolution_bitcast_fusion.2
  215.6 1.5 convolution_convert_fusion.4
  217.9 0.9 constant_dynamic-slice_fusion.4
  219.1 0.2 fusion.102
  219.6 0.7 constant_dynamic-update-slice_fusion.2
  220.4 0.9 constant_dynamic-slice_fusion.5
  221.5 0.9 convolution_bitcast_fusion.2
  222.4 1.5 convolution_convert_fusion.4
  224.7 0.9 constant_dynamic-slice_fusion.4
  226.5 0.7 constant_dynamic-update-slice_fusion.2
  227.2 0.9 constant_dynamic-slice_fusion.5
  228.3 0.9 convolution_bitcast_fusion.2
  229.2 1.5 convolution_convert_fusion.4
  231.5 0.9 constant_dynamic-slice_fusion.4
  233.3 0.7 constant_dynamic-update-slice_fusion.2
  234.0 0.9 constant_dynamic-slice_fusion.5
  235.1 0.9 convolution_bitcast_fusion.2
  236.0 1.5 convolution_convert_fusion.4
  238.3 0.9 constant_dynamic-slice_fusion.4
  239.6 0.2 fusion.102
  240.1 0.7 constant_dynamic-update-slice_fusion.2
  240.8 0.9 constant_dynamic-slice_fusion.5
  241.9 0.9 convolution_bitcast_fusion.2
  242.9 1.5 convolution_convert_fusion.4
  245.2 0.9 constant_dynamic-slice_fusion.4
  246.9 0.7 constant_dynamic-update-slice_fusion.2
  247.6 0.9 constant_dynamic-slice_fusion.5
  248.7 0.9 convolution_bitcast_fusion.2
  249.7 1.5 convolution_convert_fusion.4
  252.0 0.9 constant_dynamic-slice_fusion.4
  253.2 0.2 fusion.102
  253.7 0.7 constant_dynamic-update-slice_fusion.2
  254.5 7.1 convert_bitcast_fusion
  261.7 1.1 copy-done.1
  262.8 0.5 copy.41
  263.4 93.8 %reduce-scatter.2.cloned.1.call-done = bf16[1,512,1024]{1,2,0:T(8,128)(2,1)} async-done(((bf16[8,512,1024]{1,2,0:T(8,128)(2,1)}), bf16[1,512,1024]{1,2,0:T(8,128)(2,1)}) %reduce-scatter.2.cloned.1.call-update) | async-done | bytes 1048592 | tf_op jit(solution)/shard_map/reduce_scatter | solution.py:70
  357.1 2.4 fusion.34
  359.5 119.8 %psum.21 = f32[]{:T(128)} all-reduce(f32[]{:T(128)} %get-tuple-element.74), channel_id=1, replica_groups=mesh['dp'=8,'heads'=32] {'heads'}, use_global_device_ids=true, to_apply=%region_7.8 | all-reduce | flops 1 | bytes 8 | tf_op jit(solution)/shard_map/psum | solution.py:80
  480.0 4.4 fusion.41
  484.7 419.4 %all-reduce.3.cloned.1.call-done = bf16[512,512]{1,0:T(8,128)(2,1)} async-done(((bf16[512,512]{1,0:T(8,128)(2,1)}), bf16[512,512]{1,0:T(8,128)(2,1)}) %all-reduce.3.cloned.1.call-update) | async-done | bytes 524304 | tf_op jit(solution)/shard_map/psum | solution.py:84
  904.1 1.8 fusion.40
  906.0 3.6 multiply_add_fusion
  909.5 4.3 convolution_convert_fusion.2
  913.9 1.3 copy.46
  915.2 426.8 %all-reduce.5.cloned.1.call-done = bf16[512,512]{1,0:T(8,128)(2,1)} async-done(((bf16[512,512]{1,0:T(8,128)(2,1)}), bf16[512,512]{1,0:T(8,128)(2,1)}) %all-reduce.5.cloned.1.call-update) | async-done | bytes 524304 | tf_op jit(solution)/shard_map/psum | solution.py:84
  1342.0 1.8 fusion.39
  1343.8 4.9 multiply_bitcast_fusion
  1348.7 2.9 copy.47
  (94 shorter events, 12.8 us)
Async XLA Ops:
  12.7 187.2 %copy-start = (bf16[8,128,512]{2,1,0:T(8,128)(2,1)S(1)}, bf16[8,128,512]{2,1,0:T(8,128)(2,1)}, u32[]{:S(2)}) copy-start(bf16[8,128,512]{2,1,0:T(8,128)(2,1)} %param.8) | copy-start | bytes 3145732
  12.7 187.2 %all-to-all-start = ((bf16[8,1,512,1024]{3,2,1,0:T(8,128)(2,1)}), bf16[8,1,512,1024]{3,2,1,0:T(8,128)(2,1)}, u32[]{:S(2)}, u32[]{:S(2)}) async-start(bf16[8,1,512,1024]{3,2,1,0:T(8,128)(2,1)} %stack.2), calls=%async_computation | async-start | bytes 16777216 | tf_op jit(solution)/shard_map/all_to_all | solution.py:62
  19.5 337.7 %reduce-scatter.2.cloned.1.call-start = ((), (), s32[]{:S(2)}) async-start(), calls=%async_computation.2 | async-start | bytes 9437184 | tf_op jit(solution)/shard_map/reduce_scatter | solution.py:70
  261.6 1.2 copy-start.1
  261.6 642.5 %all-reduce.3.cloned.1.call-start = ((), (), s32[]{:S(2)}) async-start(), calls=%async_computation.3 | async-start | bytes 1048576 | tf_op jit(solution)/shard_map/psum | solution.py:84
  484.5 857.4 %all-reduce.5.cloned.1.call-start = ((), (), s32[]{:S(2)}) async-start(), calls=%async_computation.4 | async-start | bytes 1048576 | tf_op jit(solution)/shard_map/psum | solution.py:84
Sparse Core Ops, SparseCore 0:
  261.8 95.3 reduce-scatter.1
  484.6 419.4 all-reduce.2
  914.0 427.9 all-reduce.4
